TPU v7x, 128 devices: a whole 4x4x4 slice. The times are simulated.
128 devices in a mesh: lon: 32 (over y, z, x_lo), chan: 4 (over x_hi, core).
Axes of the slice: x: 4 (x_hi: 2, x_lo: 2; x = x_hi * 2 + x_lo), y: 4, z: 4, core: 2. Of those that a mesh axis runs over, the one named last changes fastest.
Arguments:
- fields: bfloat16 [1440, 49152], P('lon', 'chan'), may hold values from -6 to 6
- mix_weight: bfloat16 [384, 3456], P('chan'), may hold values from -0.109375 to 0.109375
- basis_values: float32 [5, 9, 65, 128], replicated, may hold values from -0.4 to 0.4
- source_rows: int32 [128, 5], replicated, may hold values from 0 to 131, as said below
- lon_reach: int32 [128, 5], replicated, may hold values from 1 to 32, as said below
- quad_weights: float32 [128], replicated, may hold values from 0.2 to 2
Outputs:
- spectrum: float32 [128, 552960], P('lon', 'chan')
Inputs may be any that keep to these rules, and one draw needn't show every extreme that they name: source_rows[i, e] lies between i + 4 - 4 and i + 8; entry 0 of row i is i + 4 and entry 1 is i + 4 - 4. `lon_reach`: every entry of the rows under 4 has reach 32.
All inputs are finite; a program needn't handle non-finite values.
Results may differ from a plain program's by a relative error of at most 0.005.
Values may be sent and summed in bfloat16 or wider, within the bound.
A program may use at most 128 MiB of HBM per device.

v0:
```python
import math
import jax
import jax.numpy as jnp
from jax import lax
from jax.sharding import PartitionSpec as P

C = 384
MODES = 720
K = 9
POLE = 4


def passed_along(value, axis, steps):
    count = lax.axis_size(axis)
    pairs = [(source, (source + steps) % count) for source in range(count)]
    return lax.ppermute(value, axis, pairs)


def extended(block, sides, width):
    for axis, dim in sides:
        count = lax.axis_size(axis)
        forward = [(i, i + 1) for i in range(count - 1)]
        forward.append((count - 1, 0))
        backward = [(target, source) for source, target in forward]
        low = lax.ppermute(
            lax.slice_in_dim(block, block.shape[dim] - width, None, axis=dim), axis, forward
        )
        high = lax.ppermute(lax.slice_in_dim(block, 0, width, axis=dim), axis, backward)
        block = jnp.concatenate([low, block, high], axis=dim)
    return block


def copy_for_each(value, axis):
    copies = jnp.broadcast_to(value, (lax.axis_size(axis), *value.shape))
    return lax.all_to_all(copies, axis, split_axis=0, concat_axis=0, tiled=True)


def joined_along(pieces, dim):
    shape = list(pieces.shape[1:])
    shape[dim] *= pieces.shape[0]
    return jnp.moveaxis(pieces, 0, dim).reshape(shape)


def collect(value, axis, dim):
    pieces = copy_for_each(value, axis)
    return joined_along(pieces, dim)


def extend(field, margin):
    cap_rows = field[:POLE]
    opposite = passed_along(cap_rows, "lon", lax.axis_size("lon") // 2)
    stacked = jnp.concatenate([opposite[::-1], field], axis=0)
    return extended(stacked, (("lon", 1),), margin)


def transform(block):
    length = block.shape[1]
    products = (
        jnp.arange(length, dtype=jnp.int32)[:, None]
        * jnp.arange(MODES, dtype=jnp.int32)[None, :]
        % length
    )
    angle = products.astype(jnp.float32) * (2.0 * math.pi / length)
    factor = 1.0 / math.sqrt(length)
    table = jnp.concatenate([jnp.cos(angle) * factor, -jnp.sin(angle) * factor], axis=1)
    table_high = table.astype(jnp.bfloat16)
    table_low = (table - table_high.astype(jnp.float32)).astype(jnp.bfloat16)
    first = jnp.einsum("rnc,nm->rcm", block, table_high, preferred_element_type=jnp.float32)
    second = jnp.einsum("rnc,nm->rcm", block, table_low, preferred_element_type=jnp.float32)
    return first + second


def shards(fields, mix_weight, basis_values, source_rows, lon_reach, quad_weights):
    lanes = basis_values.shape[2]
    margin = lanes // 2
    row_count = basis_values.shape[3]
    slab = fields.shape[0]
    own_channels = fields.shape[1] // row_count
    local = fields.reshape(slab, own_channels, row_count)
    padded = extend(local.transpose(2, 0, 1), margin)
    weight_whole = collect(mix_weight, "chan", 0)
    weight_cube = weight_whole.reshape(C, K, C)
    weight_part = lax.dynamic_slice_in_dim(
        weight_cube, lax.axis_index("chan") * own_channels, own_channels, 2
    )
    weight_used = weight_part.transpose(1, 2, 0)
    quad_ext = jnp.concatenate([quad_weights[:POLE][::-1], quad_weights], axis=0)
    row_quad = jnp.take(quad_ext, source_rows, axis=0)
    offsets = jnp.arange(lanes, dtype=jnp.int32) - margin
    keeping = jnp.abs(offsets)[None, None, :] <= lon_reach[:, :, None]
    basis_rows = basis_values.transpose(3, 0, 1, 2)
    weighted = basis_rows * row_quad[:, :, None, None]
    filters = jnp.where(keeping[:, :, None, :], weighted, jnp.zeros_like(weighted)).astype(
        jnp.bfloat16
    )
    padded_len = padded.shape[1]
    tap_ids = jnp.arange(lanes, dtype=jnp.int32)[:, None, None]
    source_ids = jnp.arange(padded_len, dtype=jnp.int32)[None, :, None]
    target_ids = jnp.arange(slab, dtype=jnp.int32)[None, None, :]
    selector = (source_ids - target_ids == tap_ids).astype(jnp.bfloat16)
    group = 4
    groups = row_count // group

    def one_group(index):
        start = index * group
        group_rows = lax.dynamic_slice_in_dim(source_rows, start, group, 0)
        group_filters = lax.dynamic_slice_in_dim(filters, start, group, 0)
        picked = jnp.take(padded, group_rows, axis=0)
        banded = jnp.einsum(
            "gekt,tpj->gekpj", group_filters, selector, preferred_element_type=jnp.float32
        ).astype(jnp.bfloat16)
        filtered = jnp.einsum(
            "gepc,gekpj->gkjc", picked, banded, preferred_element_type=jnp.float32
        ).astype(jnp.bfloat16)
        return jnp.einsum(
            "gkjc,kco->gjo", filtered, weight_used, preferred_element_type=jnp.float32
        )

    mixed_terms = lax.map(one_group, jnp.arange(groups, dtype=jnp.int32))
    mixed_terms = mixed_terms.reshape(row_count, slab, mixed_terms.shape[3])
    mixed = lax.psum_scatter(mixed_terms, "chan", scatter_dimension=2, tiled=True).astype(
        jnp.bfloat16
    )
    result = transform(lax.all_to_all(mixed, "lon", split_axis=0, concat_axis=1, tiled=True))
    return result.reshape(result.shape[0], result.shape[1] * result.shape[2])


def solution(mesh):
    placed = (P("lon", "chan"), P("chan", None), P(), P(), P(), P())
    return jax.shard_map(
        shards, mesh=mesh, in_specs=placed, out_specs=P("lon", "chan"), check_vma=False
    )
```

profile of v0, /device:TPU:0, one launch (start us, length us, event | category | flops | bytes accessed | tf_op | source)
XLA Modules:
  0.0 694.8 jit_solution(7724881797279448650)
XLA Ops:
  13.7 4.6 all-to-all-start
  18.9 4.3 gather_fusion.1
  24.0 4.0 rev.7
  37.6 4.8 collective-permute-start.2
  43.1 6.7 copy.78
  50.8 4.2 fusion.39
  55.0 22.2 %collective-permute-done.1 = bf16[132,32,96]{2,1,0:T(8,128)(2,1)} collective-permute-done((bf16[132,32,96]{2,1,0:T(8,128)(2,1)S(1)}, bf16[132,32,96]{2,1,0:T(8,128)(2,1)}, u32[]{:S(2)}, u32[]{:S(2)}) %collective-permute-start.1) | collective-permute-done | bytes 811040 | tf_op jit(solution)/shard_map/ppermute | solution.py:25
  80.1 16.1 %collective-permute-done.2 = bf16[132,32,96]{2,1,0:T(8,128)(2,1)} collective-permute-done((bf16[132,32,96]{2,1,0:T(8,128)(2,1)}, bf16[132,32,96]{2,1,0:T(8,128)(2,1)}, u32[]{:S(2)}, u32[]{:S(2)}) %collective-permute-start.2) | collective-permute-done | bytes 811040 | tf_op jit(solution)/shard_map/ppermute | solution.py:28
  99.1 5.8 pad_maximum_fusion.1
  104.9 8.0 %copy.90 = bf16[132,109,96]{2,1,0:T(8,128)(2,1)} copy(bf16[132,109,96]{0,2,1:T(8,128)(2,1)} %pad_maximum_fusion.1) | data formatting | bytes 5524992
  112.9 5.9 copy.88
  123.4 414.6 %while.11 = (s32[]{:T(128)}, f32[32,4,45,384]{3,2,1,0:T(8,128)}, s32[32]{0:T(128)S(1)}, bf16[128,5,9,65]{3,2,1,0:T(8,128)(2,1)}, s32[128,5]{1,0:T(8,128)}, /*ind...) while((s32[]{:T(128)}, f32[32,4,45,384]{3,2,1,0:T(8,128)}, ...), condition=%wide.region_1.2_spmd.clone, body=%wide.region_0.1_spmd.clone.sunk | while | flops 405619648 | bytes 8615271 | solution.py:119
  128.5 3.9 convolution_convert_fusion.2
  141.5 3.9 convolution_convert_fusion.2
  154.4 3.9 convolution_convert_fusion.2
  167.4 3.9 convolution_convert_fusion.2
  171.3 3.9 fusion.70
  180.3 3.9 convolution_convert_fusion.2
  193.3 3.9 convolution_convert_fusion.2
  206.2 3.9 convolution_convert_fusion.2
  210.2 4.0 fusion.70
  219.2 3.9 convolution_convert_fusion.2
  232.1 3.9 convolution_convert_fusion.2
  245.1 3.9 convolution_convert_fusion.2
  258.1 3.9 convolution_convert_fusion.2
  271.0 3.9 convolution_convert_fusion.2
  284.0 3.9 convolution_convert_fusion.2
  287.9 4.0 fusion.70
  322.8 3.9 convolution_convert_fusion.2
  387.6 3.9 convolution_convert_fusion.2
  413.5 3.9 convolution_convert_fusion.2
  426.5 3.9 convolution_convert_fusion.2
  430.4 3.9 fusion.70
  452.4 3.9 convolution_convert_fusion.2
  478.3 3.9 convolution_convert_fusion.2
  482.2 4.0 fusion.70
  491.3 3.9 convolution_convert_fusion.2
  504.2 3.9 convolution_convert_fusion.2
  508.2 3.9 fusion.70
  521.2 3.9 fusion.70
  530.2 3.9 convolution_convert_fusion.2
  538.1 9.9 %copy.92 = f32[128,45,384]{0,1,2:T(8,128)} copy(f32[128,45,384]{2,1,0:T(8,128)} %bitcast.90) | data formatting | bytes 17694720 | tf_op jit(solution)/shard_map/reshape | solution.py:120
  547.9 85.9 %reduce-scatter.2.cloned.1.call-done = f32[128,45,96]{0,1,2:T(8,128)} async-done(((f32[128,45,384]{0,1,2:T(8,128)}), f32[128,45,96]{0,1,2:T(8,128)}) %reduce-scatter.2.cloned.1.call-update) | async-done | bytes 2211856 | tf_op jit(solution)/shard_map/reduce_scatter | solution.py:121
  638.6 7.5 %all-to-all-start.1 = ((bf16[128,45,96]{2,1,0:T(8,128)(2,1)}), bf16[128,45,96]{2,1,0:T(8,128)(2,1)S(1)}, u32[]{:S(2)}, u32[]{:S(2)}) async-start(bf16[128,45,96]{2,1,0:T(8,128)(2,1)} %copy.94), calls=%async_computation.2 | async-start | bytes 3145728 | tf_op jit(solution)/shard_map/all_to_all | solution.py:124
  646.1 19.9 %negate_multiply_fusion = (f32[1440,720]{1,0:T(8,128)}, f32[1440,720]{1,0:T(8,128)}) fusion(), kind=kLoop, calls=%fused_computation.41 | loop fusion | flops 12441600 | bytes 8294400 | tf_op jit(solution)/shard_map/mul | solution.py:65
  665.9 4.6 all-to-all-done.1
  674.1 5.7 fusion.46
  679.9 4.6 fusion.51
  (283 shorter events, 320.7 us)
Async XLA Ops:
  6.5 5.5 copy-start.1
  8.6 9.7 %copy-start.2 = (s32[128,5]{0,1:T(8,128)S(1)}, s32[128,5]{0,1:T(8,128)}, u32[]{:S(2)}) copy-start(s32[128,5]{0,1:T(8,128)} %param.11) | copy-start | bytes 7684
  8.6 10.1 %copy-start.4 = (f32[128]{0:T(128)S(1)}, f32[128]{0:T(128)}, u32[]{:S(2)}) copy-start(f32[128]{0:T(128)} %param.13) | copy-start | bytes 1540
  8.6 14.8 %collective-permute-start = (bf16[4,45,96]{2,0,1:T(4,128)(2,1)S(1)}, bf16[4,45,96]{2,0,1:T(4,128)(2,1)S(1)}, u32[]{:S(2)}, u32[]{:S(2)}) collective-permute-start(bf16[4,45,96]{2,0,1:T(4,128)(2,1)S(1)} %copy.82), channel_id=1, source_target_pairs={{0,64},{4,68},{8,72},{12,76},{16,80},{20,84},{24,88},{28,92},{32,9... | collective-permute-start | bytes 103688 | tf_op jit(solution)/shard_map/ppermute | solution.py:16
  13.7 99.2 %all-to-all-start = ((bf16[4,96,3456]{2,1,0:T(8,128)(2,1)}), bf16[4,96,3456]{2,1,0:T(8,128)(2,1)}, u32[]{:S(2)}, u32[]{:S(2)}) async-start(bf16[4,96,3456]{2,1,0:T(8,128)(2,1)} %broadcast_in_dim.55), calls=%async_computation | async-start | bytes 5308416 | tf_op jit(solution)/shard_map/all_to_all | solution.py:35
  18.3 615.6 %reduce-scatter.2.cloned.1.call-start = ((), (), s32[]{:S(2)}) async-start(), calls=%async_computation.3 | async-start | bytes 11796480 | tf_op jit(solution)/shard_map/reduce_scatter | solution.py:121
  33.1 44.1 %collective-permute-start.1 = (bf16[132,32,96]{2,1,0:T(8,128)(2,1)S(1)}, bf16[132,32,96]{2,1,0:T(8,128)(2,1)}, u32[]{:S(2)}, u32[]{:S(2)}) collective-permute-start(bf16[132,32,96]{2,1,0:T(8,128)(2,1)S(1)} %copy.84), channel_id=1, source_target_pairs={{0,4},{4,8},{8,12},{12,16},{16,20},{20,24},{24,28},{28,32},{32,36}... | collective-permute-start | bytes 2433032 | tf_op jit(solution)/shard_map/ppermute | solution.py:25
  37.6 12.3 %copy-start.3 = (s32[128,5]{0,1:T(8,128)S(1)}, s32[128,5]{0,1:T(8,128)}, u32[]{:S(2)}) copy-start(s32[128,5]{0,1:T(8,128)} %param.12) | copy-start | bytes 7684
  37.6 58.6 %collective-permute-start.2 = (bf16[132,32,96]{2,1,0:T(8,128)(2,1)}, bf16[132,32,96]{2,1,0:T(8,128)(2,1)}, u32[]{:S(2)}, u32[]{:S(2)}) collective-permute-start(bf16[132,32,96]{2,1,0:T(8,128)(2,1)} %copy.85), channel_id=1, source_target_pairs={{4,0},{8,4},{12,8},{16,12},{20,16},{24,20},{28,24},{32,28},{36,32}... | collective-permute-start | bytes 2433032 | tf_op jit(solution)/shard_map/ppermute | solution.py:28
  638.6 32.0 %all-to-all-start.1 = ((bf16[128,45,96]{2,1,0:T(8,128)(2,1)}), bf16[128,45,96]{2,1,0:T(8,128)(2,1)S(1)}, u32[]{:S(2)}, u32[]{:S(2)}) async-start(bf16[128,45,96]{2,1,0:T(8,128)(2,1)} %copy.94), calls=%async_computation.2 | async-start | bytes 3145728 | tf_op jit(solution)/shard_map/all_to_all | solution.py:124
  671.5 8.4 %slice-start = ((s8[4423680]{0:T(1024)(128)(4,1)}), s8[229376]{0:T(1024)(128)(4,1)S(1)}, s32[]{:S(2)}) async-start(s8[4423680]{0:T(1024)(128)(4,1)} %bitcast.87), calls=%async_computation.4 | async-start | bytes 458752
  673.1 1.0 copy-start
  674.1 5.8 slice-start.1
Sparse Core Ops, SparseCore 0:
  548.1 85.7 reduce-scatter.1
where the time goes:
time: 701 us; the launch traced here: 695 us
  matrix products  262 us (37%)
  local copies, waits for them, and re-layouts  190 us (27%)
  waiting for transfers between devices  129 us (18%)
  other arithmetic  56.1 us (8%)
  starting transfers between devices  21.8 us (3%)
  loops' own time  21.5 us (3%)
  between operations  13.6 us (2%)
    dot_general x32, matrix products, one_group(): jnp.einsum('gekt,tpj->gekpj', group_filters, selector, preferred_element_...  126 us
    dot_general x32, matrix products, one_group(): jnp.einsum('gkjc,kco->gjo', filtered, weight_used, preferred_element_type...  126 us
    gather x64, local copies, waits for them, and re-layouts, one_group(): picked = jnp.take(padded, group_rows, axis=0)  97.4 us
    reduce_scatter x1, waiting for transfers between devices, shards(): lax.psum_scatter(mixed_terms, 'chan', scatter_dimension=2, tiled=True)  85.9 us
    and x32, other arithmetic, one_group(): picked = jnp.take(padded, group_rows, axis=0)  22.2 us
    ppermute x1, waiting for transfers between devices, extended(): lax.ppermute(lax.slice_in_dim(block, block.shape[dim] - width, None, axis...  22.2 us
    another operation x1, loops' own time, shards(): mixed_terms = lax.map(one_group, jnp.arange(groups, dtype=jnp.int32))  21.5 us
    mul x1, other arithmetic, transform(): -jnp.sin(angle) * factor  19.9 us
  transfers between devices with their start and end apart: 6, of which 4 were waited for; matrix products, arithmetic and copies ran while one was open for 10% of the time, Pallas kernels for 0%

commit v1 on v0

--- a/solution.py
+++ b/solution.py
@@ -121,7 +121,12 @@
     mixed = lax.psum_scatter(mixed_terms, "chan", scatter_dimension=2, tiled=True).astype(
         jnp.bfloat16
     )
-    result = transform(lax.all_to_all(mixed, "lon", split_axis=0, concat_axis=1, tiled=True))
+    result = transform(
+        jnp.concatenate(
+            lax.all_to_all(jnp.stack(jnp.split(mixed, lax.axis_size("lon"), axis=0)), "lon", 0, 0),
+            axis=1,
+        )
+    )
     return result.reshape(result.shape[0], result.shape[1] * result.shape[2])
 
 

time: 701 us -> 717 us (1.023)
  local copies, waits for them, and re-layouts: 190 us -> 208 us
    unnamed x19 -> x52, local copies, waits for them, and re-layouts: 18.1 us -> 38.5 us
where the time goes in v1:
time: 717 us; the launch traced here: 711 us
  matrix products  262 us (37%)
  local copies, waits for them, and re-layouts  208 us (29%)
  waiting for transfers between devices  127 us (18%)
  other arithmetic  56.2 us (8%)
  starting transfers between devices  21.9 us (3%)
  loops' own time  21.7 us (3%)
  between operations  13.6 us (2%)
    dot_general x32, matrix products, one_group(): jnp.einsum('gekt,tpj->gekpj', group_filters, selector, preferred_element_...  127 us
    dot_general x32, matrix products, one_group(): jnp.einsum('gkjc,kco->gjo', filtered, weight_used, preferred_element_type...  126 us
    gather x64, local copies, waits for them, and re-layouts, one_group(): picked = jnp.take(padded, group_rows, axis=0)  97.4 us
    reduce_scatter x1, waiting for transfers between devices, shards(): lax.psum_scatter(mixed_terms, 'chan', scatter_dimension=2, tiled=True)  86 us
    unnamed x52, local copies, waits for them, and re-layouts  38.5 us
    and x32, other arithmetic, one_group(): picked = jnp.take(padded, group_rows, axis=0)  22.2 us
    ppermute x1, waiting for transfers between devices, extended(): lax.ppermute(lax.slice_in_dim(block, block.shape[dim] - width, None, axis...  22.2 us
    another operation x1, loops' own time, shards(): mixed_terms = lax.map(one_group, jnp.arange(groups, dtype=jnp.int32))  21.7 us
  transfers between devices with their start and end apart: 6, of which 4 were waited for; matrix products, arithmetic and copies ran while one was open for 10% of the time, Pallas kernels for 0%

profile of v1, /device:TPU:0, one launch (start us, length us, event | category | flops | bytes accessed | tf_op | source)
XLA Modules:
  0.0 710.6 jit_solution(9924226695984690097)
XLA Ops:
  13.6 4.7 all-to-all-start
  18.9 4.3 gather_fusion.1
  24.1 4.0 rev.7
  37.6 4.8 collective-permute-start.2
  43.2 6.7 copy.105
  50.9 4.2 fusion.39
  55.1 22.2 %collective-permute-done.1 = bf16[132,32,96]{2,1,0:T(8,128)(2,1)} collective-permute-done((bf16[132,32,96]{2,1,0:T(8,128)(2,1)S(1)}, bf16[132,32,96]{2,1,0:T(8,128)(2,1)}, u32[]{:S(2)}, u32[]{:S(2)}) %collective-permute-start.1) | collective-permute-done | bytes 811040 | tf_op jit(solution)/shard_map/ppermute | solution.py:25
  80.2 16.1 %collective-permute-done.2 = bf16[132,32,96]{2,1,0:T(8,128)(2,1)} collective-permute-done((bf16[132,32,96]{2,1,0:T(8,128)(2,1)}, bf16[132,32,96]{2,1,0:T(8,128)(2,1)}, u32[]{:S(2)}, u32[]{:S(2)}) %collective-permute-start.2) | collective-permute-done | bytes 811040 | tf_op jit(solution)/shard_map/ppermute | solution.py:28
  99.2 5.8 pad_maximum_fusion.1
  105.0 8.0 %copy.117 = bf16[132,109,96]{2,1,0:T(8,128)(2,1)} copy(bf16[132,109,96]{0,2,1:T(8,128)(2,1)} %pad_maximum_fusion.1) | data formatting | bytes 5524992
  113.1 5.9 copy.115
  123.6 415.7 %while.11 = (s32[]{:T(128)}, f32[32,4,45,384]{3,2,1,0:T(8,128)}, s32[32]{0:T(128)S(1)}, bf16[128,5,9,65]{3,2,1,0:T(8,128)(2,1)}, s32[128,5]{1,0:T(8,128)}, /*ind...) while((s32[]{:T(128)}, f32[32,4,45,384]{3,2,1,0:T(8,128)}, ...), condition=%wide.region_1.2_spmd.clone, body=%wide.region_0.1_spmd.clone.sunk | while | flops 405619648 | bytes 8688823 | solution.py:119
  128.7 4.0 convolution_convert_fusion.2
  141.7 4.0 convolution_convert_fusion.2
  154.7 4.0 convolution_convert_fusion.2
  167.7 4.0 convolution_convert_fusion.2
  180.7 4.0 convolution_convert_fusion.2
  193.7 4.0 convolution_convert_fusion.2
  206.6 4.0 convolution_convert_fusion.2
  219.6 4.0 convolution_convert_fusion.2
  232.6 4.0 convolution_convert_fusion.2
  245.6 4.0 convolution_convert_fusion.2
  258.6 4.0 convolution_convert_fusion.2
  271.6 4.0 convolution_convert_fusion.2
  284.5 4.0 convolution_convert_fusion.2
  297.5 4.0 convolution_convert_fusion.2
  310.5 4.0 convolution_convert_fusion.2
  323.5 4.0 convolution_convert_fusion.2
  336.5 4.0 convolution_convert_fusion.2
  349.5 4.0 convolution_convert_fusion.2
  362.5 4.0 convolution_convert_fusion.2
  375.5 4.0 convolution_convert_fusion.2
  388.5 4.0 convolution_convert_fusion.2
  401.5 4.0 convolution_convert_fusion.2
  414.5 4.0 convolution_convert_fusion.2
  427.4 4.0 convolution_convert_fusion.2
  440.4 4.0 convolution_convert_fusion.2
  466.4 4.0 convolution_convert_fusion.2
  479.4 4.0 convolution_convert_fusion.2
  492.4 4.0 convolution_convert_fusion.2
  505.4 4.0 convolution_convert_fusion.2
  518.4 4.0 convolution_convert_fusion.2
  531.4 4.0 convolution_convert_fusion.2
  539.3 9.8 %copy.119 = f32[128,45,384]{0,1,2:T(8,128)} copy(f32[128,45,384]{2,1,0:T(8,128)} %bitcast.217) | data formatting | bytes 17694720 | tf_op jit(solution)/shard_map/reshape | solution.py:120
  549.0 86.0 %reduce-scatter.2.cloned.1.call-done = f32[128,45,96]{0,1,2:T(8,128)} async-done(((f32[128,45,384]{0,1,2:T(8,128)}), f32[128,45,96]{0,1,2:T(8,128)}) %reduce-scatter.2.cloned.1.call-update) | async-done | bytes 2211856 | tf_op jit(solution)/shard_map/reduce_scatter | solution.py:121
  658.0 7.5 %all-to-all-start.1 = ((bf16[32,4,45,96]{3,1,2,0:T(4,128)(2,1)}), bf16[32,4,45,96]{3,1,2,0:T(4,128)(2,1)S(1)}, u32[]{:S(2)}, u32[]{:S(2)}) async-start(bf16[32,4,45,96]{3,1,2,0:T(4,128)(2,1)} %constant_dynamic-update-slice_fusion), calls=%async_computation.2 | async-start | bytes 2949120 | tf_op jit(solution)/shard_map/all_to_all | solution.py:126
  665.5 19.9 %negate_multiply_fusion = (f32[1440,720]{1,0:T(8,128)}, f32[1440,720]{1,0:T(8,128)}) fusion(), kind=kLoop, calls=%fused_computation.41 | loop fusion | flops 12441600 | bytes 8294400 | tf_op jit(solution)/shard_map/mul | solution.py:65
  691.0 5.7 fusion.46
  (378 shorter events, 336.8 us)
Async XLA Ops:
  8.0 3.9 copy-start.3
  8.6 14.9 %collective-permute-start = (bf16[4,45,96]{2,0,1:T(4,128)(2,1)S(1)}, bf16[4,45,96]{2,0,1:T(4,128)(2,1)S(1)}, u32[]{:S(2)}, u32[]{:S(2)}) collective-permute-start(bf16[4,45,96]{2,0,1:T(4,128)(2,1)S(1)} %copy.109), channel_id=1, source_target_pairs={{0,64},{4,68},{8,72},{12,76},{16,80},{20,84},{24,88},{28,92},{32,9... | collective-permute-start | bytes 103688 | tf_op jit(solution)/shard_map/ppermute | solution.py:16
  13.6 4.8 copy-start.4
  13.6 5.1 copy-start.6
  13.6 99.4 %all-to-all-start = ((bf16[4,96,3456]{2,1,0:T(8,128)(2,1)}), bf16[4,96,3456]{2,1,0:T(8,128)(2,1)}, u32[]{:S(2)}, u32[]{:S(2)}) async-start(bf16[4,96,3456]{2,1,0:T(8,128)(2,1)} %broadcast_in_dim.55), calls=%async_computation | async-start | bytes 5308416 | tf_op jit(solution)/shard_map/all_to_all | solution.py:35
  18.4 616.7 %reduce-scatter.2.cloned.1.call-start = ((), (), s32[]{:S(2)}) async-start(), calls=%async_computation.3 | async-start | bytes 11796480 | tf_op jit(solution)/shard_map/reduce_scatter | solution.py:121
  33.2 44.1 %collective-permute-start.1 = (bf16[132,32,96]{2,1,0:T(8,128)(2,1)S(1)}, bf16[132,32,96]{2,1,0:T(8,128)(2,1)}, u32[]{:S(2)}, u32[]{:S(2)}) collective-permute-start(bf16[132,32,96]{2,1,0:T(8,128)(2,1)S(1)} %copy.111), channel_id=1, source_target_pairs={{0,4},{4,8},{8,12},{12,16},{16,20},{20,24},{24,28},{28,32},{32,36}... | collective-permute-start | bytes 2433032 | tf_op jit(solution)/shard_map/ppermute | solution.py:25
  37.6 58.6 %collective-permute-start.2 = (bf16[132,32,96]{2,1,0:T(8,128)(2,1)}, bf16[132,32,96]{2,1,0:T(8,128)(2,1)}, u32[]{:S(2)}, u32[]{:S(2)}) collective-permute-start(bf16[132,32,96]{2,1,0:T(8,128)(2,1)} %copy.112), channel_id=1, source_target_pairs={{4,0},{8,4},{12,8},{16,12},{20,16},{24,20},{28,24},{32,28},{36,32}... | collective-permute-start | bytes 2433032 | tf_op jit(solution)/shard_map/ppermute | solution.py:28
  43.2 6.8 copy-start.5
  123.6 5.1 copy-start.2
  136.6 5.1 copy-start.2
  149.6 5.1 copy-start.2
  162.6 5.1 copy-start.2
  175.6 5.1 copy-start.2
  188.6 5.1 copy-start.2
  201.5 5.1 copy-start.2
  214.5 5.1 copy-start.2
  227.5 5.1 copy-start.2
  240.5 5.1 copy-start.2
  253.5 5.1 copy-start.2
  266.5 5.1 copy-start.2
  279.4 5.1 copy-start.2
  292.4 5.1 copy-start.2
  305.4 5.1 copy-start.2
  318.4 5.1 copy-start.2
  331.4 5.1 copy-start.2
  344.4 5.1 copy-start.2
  357.4 5.1 copy-start.2
  370.4 5.1 copy-start.2
  383.4 5.1 copy-start.2
  396.4 5.1 copy-start.2
  409.4 5.1 copy-start.2
  422.4 5.1 copy-start.2
  435.4 5.1 copy-start.2
  448.3 5.1 copy-start.2
  461.3 5.1 copy-start.2
  474.3 5.1 copy-start.2
  487.3 5.1 copy-start.2
  500.3 5.1 copy-start.2
  513.3 5.1 copy-start.2
  526.3 5.1 copy-start.2
  658.0 30.4 %all-to-all-start.1 = ((bf16[32,4,45,96]{3,1,2,0:T(4,128)(2,1)}), bf16[32,4,45,96]{3,1,2,0:T(4,128)(2,1)S(1)}, u32[]{:S(2)}, u32[]{:S(2)}) async-start(bf16[32,4,45,96]{3,1,2,0:T(4,128)(2,1)} %constant_dynamic-update-slice_fusion), calls=%async_computation.2 | async-start | bytes 2949120 | tf_op jit(solution)/shard_map/all_to_all | solution.py:126
  688.3 8.4 %slice-start = ((s8[4423680]{0:T(1024)(128)(4,1)}), s8[229376]{0:T(1024)(128)(4,1)S(1)}, s32[]{:S(2)}) async-start(s8[4423680]{0:T(1024)(128)(4,1)} %bitcast.214), calls=%async_computation.4 | async-start | bytes 458752
  690.0 1.0 copy-start.1
  691.0 5.8 slice-start.1
  691.0 6.1 copy-start
Sparse Core Ops, SparseCore 0:
  549.2 85.7 reduce-scatter.1
